TPU v7x, 128 devices: a whole 4x4x4 slice. The times are simulated.
128 devices in a mesh: section: 8 (over y, core), fsdp: 16 (over x, z).
Axes of the slice: x: 4, y: 4, z: 4, core: 2. Of those that a mesh axis runs over, the one named last changes fastest.
Arguments:
- layer_input: bfloat16 [8, 8192, 2048], P('section', 'fsdp'), may hold values from -6 to 6
- resid_grad: bfloat16 [8, 8192, 2048], P('section', 'fsdp'), may hold values from -6 to 6
- qkv_grad: bfloat16 [8, 8192, 3072], P('section', 'fsdp'), may hold values from -6 to 6
- prev_input: bfloat16 [8, 8192, 2048], P('section', 'fsdp'), may hold values from -6 to 6
- prev_qkv_grad: bfloat16 [8, 8192, 3072], P('section', 'fsdp'), may hold values from -0.059814453 to 0.059814453
- qkv_weight: bfloat16 [8, 2048, 3072], P('section', 'fsdp'), may hold values from -0.125 to 0.125
- norm_gain: float32 [8, 2048], P('section'), may hold values from 0.1 to 1.9
Outputs:
- upstream_grad: bfloat16 [8, 8192, 2048], P('section', 'fsdp')
- weight_grad: float32 [8, 2048, 3072], P('section', 'fsdp')
- gain_grad: float32 [8, 2048], P('section')
All inputs are finite; a program needn't handle non-finite values.
Results may differ from a plain program's by a relative error of at most 0.018.
Values may be sent and summed in bfloat16 or wider, within the bound.
A program may use at most 128 MiB of HBM per device.

v0:
```python
import jax
import jax.numpy as jnp
from jax import lax
from jax.sharding import PartitionSpec as P

EPS = 1e-05


def from_behind(block, axis, distance):
    devices = range(lax.axis_size(axis))
    route = [(i - distance, i) for i in devices if i - distance in devices]
    return lax.ppermute(block, axis, route)


def row_scale(rows):
    values = rows.astype(jnp.float32)
    return lax.rsqrt(jnp.mean(values * values, axis=-1, keepdims=True) + EPS)


def transpose_product(grads, piece):
    return lax.dot_general(
        grads, piece, (((1,), (1,)), ((), ())), preferred_element_type=jnp.float32
    )


def local(layer_input, resid_grad, qkv_grad, prev_input, prev_qkv_grad, qkv_weight, norm_gain):
    rows_now = layer_input[0]
    grads_now = qkv_grad[0]
    rows_prev = prev_input[0]
    grads_prev = prev_qkv_grad[0]
    weight_rows = qkv_weight[0]
    gain = norm_gain[0]
    owned = weight_rows.shape[0]
    prev_scale = row_scale(rows_prev)
    prev_normed = (rows_prev.astype(jnp.float32) * prev_scale * gain[None, :]).astype(jnp.bfloat16)
    direction = transpose_product(
        grads_now, lax.all_gather(weight_rows, "fsdp", axis=0, tiled=True)
    )
    scale = row_scale(rows_now)
    values = rows_now.astype(jnp.float32)
    gained = gain[None, :] * direction
    inner = jnp.mean(gained * values, axis=-1, keepdims=True)
    local_grad = (
        resid_grad[0].astype(jnp.float32) + scale * gained - values * scale * scale * scale * inner
    ).astype(jnp.bfloat16)
    upstream_grad = from_behind(local_grad, "section", -1)
    upstream_grad, ready_rows = lax.optimization_barrier((upstream_grad, prev_normed))
    weight_grad = lax.psum_scatter(
        lax.dot_general(
            ready_rows, grads_prev, (((0,), (0,)), ((), ())), preferred_element_type=jnp.float32
        ).astype(jnp.bfloat16),
        "fsdp",
        scatter_dimension=0,
        tiled=True,
    ).astype(jnp.float32)
    owned_gain = lax.dynamic_slice_in_dim(gain, lax.axis_index("fsdp") * owned, owned, 0)
    gain_part = jnp.sum(weight_rows.astype(jnp.float32) * weight_grad, axis=1) / owned_gain
    gain_grad = lax.all_gather(gain_part, "fsdp", axis=0, tiled=True)
    return (upstream_grad[None], weight_grad[None], gain_grad[None])


def solution(mesh):
    placed = (
        P("section", "fsdp", None),
        P("section", "fsdp", None),
        P("section", "fsdp", None),
        P("section", "fsdp", None),
        P("section", "fsdp", None),
        P("section", "fsdp", None),
        P("section", None),
    )
    return jax.shard_map(
        local,
        mesh=mesh,
        in_specs=placed,
        out_specs=(P("section", "fsdp", None), P("section", "fsdp", None), P("section", None)),
        check_vma=False,
    )
```

profile of v0, /device:TPU:0, one launch (start us, length us, event | category | flops | bytes accessed | tf_op | source)
XLA Modules:
  0.0 288.5 jit_solution(17675918492956940125)
XLA Ops:
  7.2 0.0 copy-start
  7.2 0.0 all-gather.4.cloned.1.call-start
  7.2 0.7 all-gather.4.cloned.1.call-update
  7.9 0.0 reduce-scatter.2.cloned.1.call-start
  8.0 2.2 fusion.2
  10.2 92.6 %all-gather.4.cloned.1.call-done = bf16[1,2048,3072]{2,1,0:T(8,128)(2,1)} async-done(((bf16[1,128,3072]{2,1,0:T(8,128)(2,1)}), bf16[1,2048,3072]{2,1,0:T(8,128)(2,1)}) %all-gather.4.cloned.1.call-update) | async-done | bytes 12582928 | tf_op jit(solution)/shard_map/all_gather | solution.py:37
  102.8 0.0 copy-start.1
  102.8 15.5 %fusion.5 = (f32[512]{0:T(512)S(1)}, f32[512]{0:T(512)S(1)}, bf16[512,2048]{1,0:T(8,128)(2,1)}, f32[512,2048]{1,0:T(8,128)}) fusion(bf16[1,512,2048]{2,1,0:T(8,128)(2,1)} %param.7, f32[2048]{0:T(1024)} %bitcast.41, f32[512]{0:T(512)S(1)} %add_rsqrt_fusion, bf16[1,512,2048]{2,1,0:T(8,128)(2,1)} %param.10, ...), kind=kOutput, calls=%fused_computation.11 | convolution fusion | flops 6452935680 | bytes 26228736 | tf_op jit(solution)/shard_map/dot_general | solution.py:21
  118.3 0.0 copy-done.1
  118.3 0.0 copy-start.2
  118.4 5.3 %fusion.10 = bf16[512,2048]{1,0:T(8,128)(2,1)S(1)} fusion(f32[512,2048]{1,0:T(8,128)} %get-tuple-element.10, bf16[1,512,2048]{2,1,0:T(8,128)(2,1)} %param.8, bf16[1,512,2048]{2,1,0:T(8,128)(2,1)} %param.7, f32[512]{0:T(512)S(1)} %get-tuple-element.12, f32[2048]{0:T(1024)S(1)} %bitcast.42, f32[512]{0:T(512)S(1)} %get-tuple-element.11), kind=kLoop, calls=%fused_computation.16 | loop fusion | flops 11534336 | bytes 10498048 | tf_op jit(solution)/shard_map/convert_element_type | solution.py:45
  123.6 1.3 collective-permute-start
  124.9 4.9 %collective-permute-done = bf16[512,2048]{1,0:T(8,128)(2,1)} collective-permute-done((bf16[512,2048]{1,0:T(8,128)(2,1)S(1)}, bf16[512,2048]{1,0:T(8,128)(2,1)}, u32[]{:S(2)}, u32[]{:S(2)}) %collective-permute-start) | collective-permute-done | bytes 2097184 | tf_op jit(solution)/shard_map/ppermute | solution.py:12
  129.8 0.0 copy-done
  129.8 0.0 copy-done.2
  129.8 9.7 %convolution_convert_fusion = bf16[2048,3072]{1,0:T(8,128)(2,1)} fusion(bf16[512,2048]{1,0:T(8,128)(2,1)S(1)} %copy-done.2, bf16[1,512,3072]{2,1,0:T(8,128)(2,1)S(1)} %copy-done), kind=kOutput, calls=%fused_computation.2 | convolution fusion | flops 6448742400 | bytes 17825792 | tf_op jit(solution)/shard_map/dot_general | solution.py:49
  139.5 0.0 reduce-scatter.2.cloned.1.call-update
  139.6 114.9 %reduce-scatter.2.cloned.1.call-done = bf16[128,3072]{1,0:T(8,128)(2,1)} async-done(((bf16[2048,3072]{1,0:T(8,128)(2,1)}), bf16[128,3072]{1,0:T(8,128)(2,1)}) %reduce-scatter.2.cloned.1.call-update) | async-done | bytes 786448 | tf_op jit(solution)/shard_map/reduce_scatter | solution.py:48
  254.4 1.7 fusion.14
  256.1 19.3 %all-gather.1 = f32[16,1,128]{2,1,0:T(1,128)S(1)} all-gather(f32[1,1,128]{2,1,0:T(1,128)S(1)} %fusion.15), channel_id=1, replica_groups=mesh['section'=8,'fsdp'=16] {'fsdp'}, dimensions={0}, use_global_device_ids=true | all-gather | bytes 8704 | tf_op jit(solution)/shard_map/all_gather | solution.py:58
  275.4 2.4 convert_bitcast_fusion
  277.9 3.2 %copy.12 = bf16[1,512,2048]{2,1,0:T(8,128)(2,1)} copy(bf16[1,512,2048]{2,1,0:T(8,128)(2,1)} %bitcast.8) | data formatting | bytes 4194304
  281.0 0.6 copy.13
  (3 shorter events, 0.0 us)
Async XLA Ops:
  7.2 122.7 %copy-start = (bf16[1,512,3072]{2,1,0:T(8,128)(2,1)S(1)}, bf16[1,512,3072]{2,1,0:T(8,128)(2,1)}, u32[]{:S(2)}) copy-start(bf16[1,512,3072]{2,1,0:T(8,128)(2,1)} %param.11) | copy-start | bytes 9437188
  7.2 95.7 %all-gather.4.cloned.1.call-start = ((), (), s32[]{:S(2)}) async-start(), calls=%async_computation.2 | async-start | bytes 13369344 | tf_op jit(solution)/shard_map/all_gather | solution.py:37
  7.9 246.5 %reduce-scatter.2.cloned.1.call-start = ((), (), s32[]{:S(2)}) async-start(), calls=%async_computation.1 | async-start | bytes 13369344 | tf_op jit(solution)/shard_map/reduce_scatter | solution.py:48
  102.8 15.5 %copy-start.1 = (f32[1,2048]{1,0:T(1,128)S(1)}, f32[1,2048]{1,0:T(1,128)}, u32[]{:S(2)}) copy-start(f32[1,2048]{1,0:T(1,128)} %param.13) | copy-start | bytes 24580
  118.3 11.5 %copy-start.2 = (bf16[512,2048]{1,0:T(8,128)(2,1)S(1)}, bf16[512,2048]{1,0:T(8,128)(2,1)}, u32[]{:S(2)}) copy-start(bf16[512,2048]{1,0:T(8,128)(2,1)} %get-tuple-element.6) | copy-start | bytes 6291460
  123.6 6.2 %collective-permute-start = (bf16[512,2048]{1,0:T(8,128)(2,1)S(1)}, bf16[512,2048]{1,0:T(8,128)(2,1)}, u32[]{:S(2)}, u32[]{:S(2)}) collective-permute-start(bf16[512,2048]{1,0:T(8,128)(2,1)S(1)} %fusion.10), channel_id=1, source_target_pairs={{16,0},{32,16},{48,32},{64,48},{80,64},{96,80},{112,96},{17,1},{33... | collective-permute-start | bytes 6291464 | tf_op jit(solution)/shard_map/ppermute | solution.py:12
Sparse Core Ops, SparseCore 0:
  10.2 92.5 all-gather.3
  139.7 114.6 reduce-scatter.1
where the time goes:
time: 289 us; the launch traced here: 288 us
  waiting for transfers between devices  213 us (74%)
  matrix products  25.2 us (9%)
  blocking collectives  19.3 us (7%)
  between operations  14.1 us (5%)
  other arithmetic  11.6 us (4%)
  local copies, waits for them, and re-layouts  3.78 us (1%)
    reduce_scatter x1, waiting for transfers between devices, local(): lax.psum_scatter(lax.dot_general(ready_rows, grads_prev, (((0,), (0,)), (...  115 us
    all_gather x1, waiting for transfers between devices, local(): lax.all_gather(weight_rows, 'fsdp', axis=0, tiled=True)  92.6 us
    all_gather x1, blocking collectives, local(): gain_grad = lax.all_gather(gain_part, 'fsdp', axis=0, tiled=True)  19.3 us
    dot_general x1, matrix products, transpose_product(): lax.dot_general(grads, piece, (((1,), (1,)), ((), ())), preferred_element...  15.5 us
    dot_general x1, matrix products, local(): lax.dot_general(ready_rows, grads_prev, (((0,), (0,)), ((), ())), preferr...  9.72 us
  transfers between devices with their start and end apart: 3, of which 3 were waited for; matrix products, arithmetic and copies ran while one was open for 1% of the time, Pallas kernels for 0%

commit v1 on v0

--- a/solution.py
+++ b/solution.py
@@ -55,7 +55,9 @@
     ).astype(jnp.float32)
     owned_gain = lax.dynamic_slice_in_dim(gain, lax.axis_index("fsdp") * owned, owned, 0)
     gain_part = jnp.sum(weight_rows.astype(jnp.float32) * weight_grad, axis=1) / owned_gain
-    gain_grad = lax.all_gather(gain_part, "fsdp", axis=0, tiled=True)
+    gain_grad = jnp.concatenate(
+        lax.all_to_all(jnp.stack([gain_part] * lax.axis_size("fsdp")), "fsdp", 0, 0), axis=0
+    )
     return (upstream_grad[None], weight_grad[None], gain_grad[None])
 
 

time: 289 us -> 280 us (0.969)
  blocking collectives: 19.3 us -> 0 us
  waiting for transfers between devices: 213 us -> 218 us
  starting transfers between devices: 1.37 us -> 5.98 us
    all_gather x1 -> x0, blocking collectives: 19.3 us -> none  [local(): gain_grad = lax.all_gather(gain_part, 'fsdp', axis=0, tiled=True)]
    all_to_all x0 -> x1, waiting for transfers between devices: none -> 5.05 us  [local(): lax.all_to_all(jnp.stack([gain_part] * lax.axis_size('fsdp')), 'fsdp', 0, 0)]
    all_to_all x0 -> x1, starting transfers between devices: none -> 4.62 us  [local(): lax.all_to_all(jnp.stack([gain_part] * lax.axis_size('fsdp')), 'fsdp', 0, 0)]
  transfers between devices with their start and end apart: 3 -> 4, of which waited for: 3 -> 4; matrix products, arithmetic and copies ran while one was open for 1% -> 2% of each run, Pallas kernels for 0% -> 0%
where the time goes in v1:
time: 280 us; the launch traced here: 279 us
  waiting for transfers between devices  218 us (78%)
  matrix products  25.2 us (9%)
  between operations  14.1 us (5%)
  other arithmetic  11.6 us (4%)
  starting transfers between devices  5.98 us (2%)
  local copies, waits for them, and re-layouts  4.38 us (2%)
    reduce_scatter x1, waiting for transfers between devices, local(): lax.psum_scatter(lax.dot_general(ready_rows, grads_prev, (((0,), (0,)), (...  115 us
    all_gather x1, waiting for transfers between devices, local(): lax.all_gather(weight_rows, 'fsdp', axis=0, tiled=True)  92.6 us
    dot_general x1, matrix products, transpose_product(): lax.dot_general(grads, piece, (((1,), (1,)), ((), ())), preferred_element...  15.5 us
    dot_general x1, matrix products, local(): lax.dot_general(ready_rows, grads_prev, (((0,), (0,)), ((), ())), preferr...  9.72 us
  transfers between devices with their start and end apart: 4, of which 4 were waited for; matrix products, arithmetic and copies ran while one was open for 2% of the time, Pallas kernels for 0%

profile of v1, /device:TPU:0, one launch (start us, length us, event | category | flops | bytes accessed | tf_op | source)
XLA Modules:
  0.0 279.4 jit_solution(3791839593174945489)
XLA Ops:
  7.2 0.0 copy-start
  7.2 0.0 all-gather.3.cloned.1.call-start
  7.2 0.7 all-gather.3.cloned.1.call-update
  7.9 0.0 reduce-scatter.2.cloned.1.call-start
  8.0 2.2 fusion.2
  10.2 92.6 %all-gather.3.cloned.1.call-done = bf16[1,2048,3072]{2,1,0:T(8,128)(2,1)} async-done(((bf16[1,128,3072]{2,1,0:T(8,128)(2,1)}), bf16[1,2048,3072]{2,1,0:T(8,128)(2,1)}) %all-gather.3.cloned.1.call-update) | async-done | bytes 12582928 | tf_op jit(solution)/shard_map/all_gather | solution.py:37
  102.8 15.5 %fusion.5 = (f32[512]{0:T(512)S(1)}, f32[512]{0:T(512)S(1)}, bf16[512,2048]{1,0:T(8,128)(2,1)}, f32[512,2048]{1,0:T(8,128)}) fusion(bf16[1,512,2048]{2,1,0:T(8,128)(2,1)} %param.7, f32[2048]{0:T(1024)} %bitcast.41, f32[512]{0:T(512)S(1)} %add_rsqrt_fusion, bf16[1,512,2048]{2,1,0:T(8,128)(2,1)} %param.10, ...), kind=kOutput, calls=%fused_computation.11 | convolution fusion | flops 6452935680 | bytes 26228736 | tf_op jit(solution)/shard_map/dot_general | solution.py:21
  118.3 0.0 copy-done.1
  118.3 0.0 copy-start.2
  118.4 5.3 %fusion.10 = bf16[512,2048]{1,0:T(8,128)(2,1)S(1)} fusion(f32[512,2048]{1,0:T(8,128)} %get-tuple-element.10, bf16[1,512,2048]{2,1,0:T(8,128)(2,1)} %param.8, bf16[1,512,2048]{2,1,0:T(8,128)(2,1)} %param.7, f32[512]{0:T(512)S(1)} %get-tuple-element.12, f32[2048]{0:T(1024)S(1)} %bitcast.42, f32[512]{0:T(512)S(1)} %get-tuple-element.11), kind=kLoop, calls=%fused_computation.16 | loop fusion | flops 11534336 | bytes 10498048 | tf_op jit(solution)/shard_map/convert_element_type | solution.py:45
  123.6 1.3 collective-permute-start
  124.9 4.9 %collective-permute-done = bf16[512,2048]{1,0:T(8,128)(2,1)} collective-permute-done((bf16[512,2048]{1,0:T(8,128)(2,1)S(1)}, bf16[512,2048]{1,0:T(8,128)(2,1)}, u32[]{:S(2)}, u32[]{:S(2)}) %collective-permute-start) | collective-permute-done | bytes 2097184 | tf_op jit(solution)/shard_map/ppermute | solution.py:12
  129.8 0.0 copy-done
  129.8 0.0 copy-done.2
  129.8 9.7 %convolution_convert_fusion = bf16[2048,3072]{1,0:T(8,128)(2,1)} fusion(bf16[512,2048]{1,0:T(8,128)(2,1)S(1)} %copy-done.2, bf16[1,512,3072]{2,1,0:T(8,128)(2,1)S(1)} %copy-done), kind=kOutput, calls=%fused_computation.2 | convolution fusion | flops 6448742400 | bytes 17825792 | tf_op jit(solution)/shard_map/dot_general | solution.py:49
  139.5 0.0 reduce-scatter.2.cloned.1.call-update
  139.6 114.9 %reduce-scatter.2.cloned.1.call-done = bf16[128,3072]{1,0:T(8,128)(2,1)} async-done(((bf16[2048,3072]{1,0:T(8,128)(2,1)}), bf16[128,3072]{1,0:T(8,128)(2,1)}) %reduce-scatter.2.cloned.1.call-update) | async-done | bytes 786448 | tf_op jit(solution)/shard_map/reduce_scatter | solution.py:48
  254.4 1.7 fusion.14
  256.1 0.6 stack.2
  256.7 4.6 %all-to-all-start = ((f32[16,1,128]{2,1,0:T(1,128)}), f32[16,1,128]{2,1,0:T(1,128)S(1)}, u32[]{:S(2)}, u32[]{:S(2)}) async-start(f32[16,1,128]{2,1,0:T(1,128)} %stack.2), calls=%async_computation.1 | async-start | bytes 16384 | tf_op jit(solution)/shard_map/all_to_all | solution.py:59
  261.3 2.4 convert_bitcast_fusion
  263.8 5.1 %all-to-all-done = f32[16,1,128]{2,1,0:T(1,128)S(1)} async-done(((f32[16,1,128]{2,1,0:T(1,128)}), f32[16,1,128]{2,1,0:T(1,128)S(1)}, u32[]{:S(2)}, u32[]{:S(2)}) %all-to-all-start) | async-done | bytes 8224 | tf_op jit(solution)/shard_map/all_to_all | solution.py:59
  268.8 3.2 %copy.12 = bf16[1,512,2048]{2,1,0:T(8,128)(2,1)} copy(bf16[1,512,2048]{2,1,0:T(8,128)(2,1)} %bitcast.8) | data formatting | bytes 4194304
  272.0 0.6 copy.13
  (4 shorter events, 0.0 us)
Async XLA Ops:
  7.2 122.7 %copy-start = (bf16[1,512,3072]{2,1,0:T(8,128)(2,1)S(1)}, bf16[1,512,3072]{2,1,0:T(8,128)(2,1)}, u32[]{:S(2)}) copy-start(bf16[1,512,3072]{2,1,0:T(8,128)(2,1)} %param.11) | copy-start | bytes 9437188
  7.2 95.7 %all-gather.3.cloned.1.call-start = ((), (), s32[]{:S(2)}) async-start(), calls=%async_computation.3 | async-start | bytes 13369344 | tf_op jit(solution)/shard_map/all_gather | solution.py:37
  7.9 246.5 %reduce-scatter.2.cloned.1.call-start = ((), (), s32[]{:S(2)}) async-start(), calls=%async_computation.2 | async-start | bytes 13369344 | tf_op jit(solution)/shard_map/reduce_scatter | solution.py:48
  102.8 15.5 %copy-start.1 = (f32[1,2048]{1,0:T(1,128)S(1)}, f32[1,2048]{1,0:T(1,128)}, u32[]{:S(2)}) copy-start(f32[1,2048]{1,0:T(1,128)} %param.13) | copy-start | bytes 24580
  118.3 11.5 %copy-start.2 = (bf16[512,2048]{1,0:T(8,128)(2,1)S(1)}, bf16[512,2048]{1,0:T(8,128)(2,1)}, u32[]{:S(2)}) copy-start(bf16[512,2048]{1,0:T(8,128)(2,1)} %get-tuple-element.6) | copy-start | bytes 6291460
  123.6 6.2 %collective-permute-start = (bf16[512,2048]{1,0:T(8,128)(2,1)S(1)}, bf16[512,2048]{1,0:T(8,128)(2,1)}, u32[]{:S(2)}, u32[]{:S(2)}) collective-permute-start(bf16[512,2048]{1,0:T(8,128)(2,1)S(1)} %fusion.10), channel_id=1, source_target_pairs={{16,0},{32,16},{48,32},{64,48},{80,64},{96,80},{112,96},{17,1},{33... | collective-permute-start | bytes 6291464 | tf_op jit(solution)/shard_map/ppermute | solution.py:12
  256.7 12.1 %all-to-all-start = ((f32[16,1,128]{2,1,0:T(1,128)}), f32[16,1,128]{2,1,0:T(1,128)S(1)}, u32[]{:S(2)}, u32[]{:S(2)}) async-start(f32[16,1,128]{2,1,0:T(1,128)} %stack.2), calls=%async_computation.1 | async-start | bytes 16384 | tf_op jit(solution)/shard_map/all_to_all | solution.py:59
Sparse Core Ops, SparseCore 0:
  10.2 92.5 all-gather.2
  139.7 114.6 reduce-scatter.1
